TPU v7x, 32 devices: a whole 2x2x4 slice. The times are simulated.
32 devices in a mesh: dp: 4 (over x, core), ctx: 8 (over z, y).
Axes of the slice: x: 2, y: 2, z: 4, core: 2. Of those that a mesh axis runs over, the one named last changes fastest.
Arguments:
- queries: bfloat16 [4, 2048, 1024], P('dp', 'ctx'), may hold values from -4.5 to 4.5
- keys: bfloat16 [4, 2048, 1024], P('dp', 'ctx'), may hold values from -4.5 to 4.5
- values: bfloat16 [4, 2048, 1024], P('dp', 'ctx'), may hold values from -6 to 6
- out_grad: bfloat16 [4, 2048, 2048], P('dp', 'ctx'), may hold values from -6 to 6
- chosen: int32 [4, 8], P('dp'), may hold values from -1 to 15, as said below
- proj: bfloat16 [1024, 2048], P('ctx', 'dp'), may hold values from -0.1875 to 0.1875
Outputs:
- attn_out: bfloat16 [4, 2048, 2048], P('dp', 'ctx')
- q_grad: bfloat16 [4, 2048, 1024], P('dp', 'ctx')
- k_grad: bfloat16 [4, 2048, 1024], P('dp', 'ctx')
- v_grad: bfloat16 [4, 2048, 1024], P('dp', 'ctx')
- proj_grad: float32 [1024, 2048], P('ctx', 'dp')
Inputs may be any that keep to these rules, and one draw needn't show every extreme that they name: chosen[d, c] is -1 or the index pos // 128 of one of the blocks that ctx index c stores (position spans c and 15 - c, of 1 block each); every sequence has one or more entries that are not -1.
All inputs are finite; a program needn't handle non-finite values.
Results may differ from a plain program's by a relative error of at most 0.023.
Values may be sent and summed in bfloat16 or wider, within the bound.
A program may use at most 192 MiB of HBM per device.

v0:
```python
import math
import jax
import jax.numpy as jnp
from jax import lax
from jax.sharding import PartitionSpec as P

BLOCK = 128


def cross_dot(left_op, right_op):
    return lax.dot_general(
        left_op, right_op, (((1,), (1,)), ((), ())), preferred_element_type=jnp.float32
    )


def inner_dot(left_op, right_op):
    return lax.dot_general(
        left_op, right_op, (((0,), (0,)), ((), ())), preferred_element_type=jnp.float32
    )


def head_probs(
    query_block,
    query_pos,
    query_live,
    query_ids,
    heads_k,
    slot_pos,
    slot_live,
    slot_ids,
    score_scale,
):
    scores = cross_dot(query_block, heads_k) * score_scale
    allowed = query_live[:, None] & slot_live[None, :] & (
        slot_pos[None, :] <= query_pos[:, None]
    ) | (query_ids[:, None] == slot_ids[None, :])
    masked = jnp.where(allowed, scores, -1e30)
    row_max = jnp.max(masked, axis=1, keepdims=True)
    exp_terms = jnp.where(allowed, jnp.exp(masked - row_max), 0.0)
    return exp_terms / jnp.sum(exp_terms, axis=1, keepdims=True)


def shards(queries, keys, values, out_grad, chosen, proj):
    ctx_count = lax.axis_size("ctx")
    ctx_index = lax.axis_index("ctx")
    tokens = queries.shape[1]
    half_rows = tokens // 2
    block_rows = BLOCK
    picked = chosen[0]
    own_pick = lax.dynamic_index_in_dim(picked, ctx_index, 0, keepdims=False)
    own_live = own_pick >= 0
    first_pos = jnp.where(own_live, own_pick, 0) * block_rows
    local_row = jnp.where(
        first_pos // half_rows == ctx_index,
        first_pos % half_rows,
        half_rows + first_pos % half_rows,
    )
    row_start = jnp.where(own_live, local_row, 0)

    def take_rows(source):
        slot_block = lax.dynamic_slice_in_dim(source[0], row_start, block_rows, 0)
        return jnp.where(own_live, slot_block, jnp.zeros((), source.dtype))

    def place_rows(slot_block, template):
        return lax.dynamic_update_slice_in_dim(
            jnp.zeros(template.shape, jnp.bfloat16), slot_block[None], row_start, 1
        )

    q_slot = take_rows(queries)
    k_slot = take_rows(keys)
    v_slot = take_rows(values)
    g_slot = take_rows(out_grad)
    heads_q, heads_k, heads_v = (
        lax.all_to_all(q_slot, "ctx", split_axis=1, concat_axis=0, tiled=True),
        lax.all_to_all(k_slot, "ctx", split_axis=1, concat_axis=0, tiled=True),
        lax.all_to_all(v_slot, "ctx", split_axis=1, concat_axis=0, tiled=True),
    )
    slot_count = ctx_count * block_rows
    offsets = jnp.arange(block_rows, dtype=jnp.int32)
    safe_pick = jnp.where(picked >= 0, picked, 0)
    slot_pos = (safe_pick[:, None] * block_rows + offsets[None, :]).reshape(slot_count)
    slot_live = jnp.repeat(picked >= 0, block_rows)
    slot_ids = jnp.arange(slot_count, dtype=jnp.int32)
    head_dim = heads_q.shape[1]
    score_scale = 1.0 / math.sqrt(head_dim)
    step_rows = min(512, slot_count)
    step_count = slot_count // step_rows
    attn_parts = []
    prob_store = []
    prob_b_store = []
    for step_index in range(step_count):
        row_low = step_index * step_rows
        window = slice(row_low, row_low + step_rows)
        attn_prob = head_probs(
            heads_q[window],
            slot_pos[window],
            slot_live[window],
            slot_ids[window],
            heads_k,
            slot_pos,
            slot_live,
            slot_ids,
            score_scale,
        )
        prob_b = attn_prob.astype(jnp.bfloat16)
        prob_store.append(attn_prob)
        prob_b_store.append(prob_b)
        attn_parts.append(
            jnp.dot(prob_b, heads_v, preferred_element_type=jnp.float32).astype(jnp.bfloat16)
        )
    attn_heads = jnp.concatenate(attn_parts, 0)
    attn_local = lax.all_to_all(attn_heads, "ctx", split_axis=0, concat_axis=1, tiled=True)
    head_rows = lax.all_gather(proj, "dp", axis=1, tiled=True)
    full_proj = lax.all_gather(head_rows, "ctx", axis=0, tiled=True)
    mixed = jnp.dot(attn_local, full_proj, preferred_element_type=jnp.float32).astype(jnp.bfloat16)
    attn_out = place_rows(mixed, out_grad)
    part_rows = lax.all_gather(g_slot, "ctx", axis=0, tiled=True)
    weight_term = inner_dot(attn_heads, part_rows)
    rows_grad = cross_dot(part_rows, head_rows)
    weight_term, rows_grad = (weight_term, rows_grad)
    attn_grad = rows_grad.astype(jnp.bfloat16)
    proj_grad = lax.psum_scatter(weight_term, "dp", scatter_dimension=1, tiled=True)
    key_grad = jnp.zeros((slot_count, head_dim), jnp.float32)
    value_grad = jnp.zeros((slot_count, head_dim), jnp.float32)
    query_parts = []
    for step_index in range(step_count):
        row_low = step_index * step_rows
        window = slice(row_low, row_low + step_rows)
        attn_prob = prob_store[step_index]
        prob_b = prob_b_store[step_index]
        grad_block = attn_grad[window]
        row_delta = jnp.sum(
            grad_block.astype(jnp.float32) * attn_heads[window].astype(jnp.float32),
            axis=1,
            keepdims=True,
        )
        score_grad = (attn_prob * (cross_dot(grad_block, heads_v) - row_delta)).astype(jnp.bfloat16)
        query_parts.append(
            (jnp.dot(score_grad, heads_k, preferred_element_type=jnp.float32) * score_scale).astype(
                jnp.bfloat16
            )
        )
        key_grad = key_grad + inner_dot(score_grad, heads_q[window])
        value_grad = value_grad + inner_dot(prob_b, grad_block)
    q_heads_grad = jnp.concatenate(query_parts, 0)
    k_heads_grad = (key_grad * score_scale).astype(jnp.bfloat16)
    v_heads_grad = value_grad.astype(jnp.bfloat16)
    q_back, k_back, v_back = (
        lax.all_to_all(q_heads_grad, "ctx", split_axis=0, concat_axis=1, tiled=True),
        lax.all_to_all(k_heads_grad, "ctx", split_axis=0, concat_axis=1, tiled=True),
        lax.all_to_all(v_heads_grad, "ctx", split_axis=0, concat_axis=1, tiled=True),
    )
    return (
        attn_out,
        place_rows(q_back, queries),
        place_rows(k_back, keys),
        place_rows(v_back, values),
        proj_grad,
    )


def solution(mesh):
    placed = (
        P("dp", "ctx", None),
        P("dp", "ctx", None),
        P("dp", "ctx", None),
        P("dp", "ctx", None),
        P("dp", None),
        P("ctx", "dp"),
    )
    return jax.shard_map(
        shards,
        mesh=mesh,
        in_specs=placed,
        out_specs=(
            P("dp", "ctx", None),
            P("dp", "ctx", None),
            P("dp", "ctx", None),
            P("dp", "ctx", None),
            P("ctx", "dp"),
        ),
        check_vma=False,
    )
```

profile of v0, /device:TPU:0, one launch (start us, length us, event | category | flops | bytes accessed | tf_op | source)
XLA Modules:
  0.0 224.0 jit_solution(12597363358342801564)
XLA Ops:
  9.9 2.0 dynamic-slice_select_fusion
  12.0 10.2 %all_gather.9 = bf16[128,2048]{1,0:T(8,128)(2,1)} all-gather(bf16[128,512]{1,0:T(8,128)(2,1)} %param.11), channel_id=1, replica_groups=mesh['dp'=4,'ctx'=8] {'dp'}, dimensions={1}, use_global_device_ids=true | all-gather | bytes 655360 | tf_op jit(solution)/shard_map/all_gather | solution.py:113
  23.4 5.8 %all-to-all-start.1 = ((bf16[128,8,128]{0,2,1:T(8,128)(2,1)}), bf16[128,8,128]{0,2,1:T(8,128)(2,1)S(1)}, u32[]{:S(2)}, u32[]{:S(2)}) async-start(bf16[128,8,128]{0,2,1:T(8,128)(2,1)} %bitcast.9), calls=%async_computation.1 | async-start | bytes 524288 | tf_op jit(solution)/shard_map/all_to_all | solution.py:75
  30.6 15.6 %all-to-all-done.1 = bf16[128,8,128]{0,2,1:T(8,128)(2,1)S(1)} async-done(((bf16[128,8,128]{0,2,1:T(8,128)(2,1)}), bf16[128,8,128]{0,2,1:T(8,128)(2,1)S(1)}, u32[]{:S(2)}, u32[]{:S(2)}) %all-to-all-start.1) | async-done | bytes 262176 | tf_op jit(solution)/shard_map/all_to_all | solution.py:75
  46.3 3.5 %all-to-all-start = ((bf16[128,8,128]{0,2,1:T(8,128)(2,1)}), bf16[128,8,128]{0,2,1:T(8,128)(2,1)S(1)}, u32[]{:S(2)}, u32[]{:S(2)}) async-start(bf16[128,8,128]{0,2,1:T(8,128)(2,1)} %bitcast.6), calls=%async_computation | async-start | bytes 524288 | tf_op jit(solution)/shard_map/all_to_all | solution.py:74
  50.5 12.3 %all-to-all-done = bf16[128,8,128]{0,2,1:T(8,128)(2,1)S(1)} async-done(((bf16[128,8,128]{0,2,1:T(8,128)(2,1)}), bf16[128,8,128]{0,2,1:T(8,128)(2,1)S(1)}, u32[]{:S(2)}, u32[]{:S(2)}) %all-to-all-start) | async-done | bytes 262176 | tf_op jit(solution)/shard_map/all_to_all | solution.py:74
  62.8 5.5 %all-to-all-start.2 = ((bf16[128,8,128]{0,2,1:T(8,128)(2,1)}), bf16[128,8,128]{0,2,1:T(8,128)(2,1)S(1)}, u32[]{:S(2)}, u32[]{:S(2)}) async-start(bf16[128,8,128]{0,2,1:T(8,128)(2,1)} %bitcast.12), calls=%async_computation.2 | async-start | bytes 524288 | tf_op jit(solution)/shard_map/all_to_all | solution.py:76
  68.9 15.9 %all-to-all-done.2 = bf16[128,8,128]{0,2,1:T(8,128)(2,1)S(1)} async-done(((bf16[128,8,128]{0,2,1:T(8,128)(2,1)}), bf16[128,8,128]{0,2,1:T(8,128)(2,1)S(1)}, u32[]{:S(2)}, u32[]{:S(2)}) %all-to-all-start.2) | async-done | bytes 262176 | tf_op jit(solution)/shard_map/all_to_all | solution.py:76
  87.3 3.0 %fusion.11 = (f32[512]{0:T(512)S(1)}, f32[512]{0:T(512)S(1)}) fusion(f32[512,1024]{1,0:T(8,128)S(1)} %get-tuple-element.21, f32[512]{0:T(512)S(1)} %get-tuple-element.9, s32[512]{0:T(512)S(1)} %slice.46, s32[512]{0:T(512)S(1)} %get-tuple-element.16, s32[1024]{0:T(1024)S(1)} %get-tuple-element.19, pred[1024]{0:T(1024)(128)(4,1)S(1)} %broadcast_bitcast_fusion, ...), kind=kLoop, calls=%fused_computation.22 | loop fusion | flops 10484736 | bytes 4216832 | tf_op jit(solution)/shard_map/reduce_sum | solution.py:40
  90.4 3.8 %fusion.10 = (f32[512,1024]{1,0:T(8,128)}, f32[512,1024]{1,0:T(8,128)S(1)}) fusion(f32[512,1024]{1,0:T(8,128)S(1)} %get-tuple-element.21, f32[512]{0:T(512)S(1)} %get-tuple-element.7, f32[512]{0:T(512)S(1)} %get-tuple-element.9, s32[512]{0:T(512)S(1)} %slice.46, s32[512]{0:T(512)S(1)} %get-tuple-element.16, s32[1024]{0:T(1024)S(1)} %get-tuple-element.19, ...), kind=kLoop, calls=%fused_computation.21 | loop fusion | flops 10485760 | bytes 8411136 | tf_op jit(solution)/shard_map/div | solution.py:40
  94.6 4.0 %all-gather.6.cloned.1.call-done = bf16[1,1024,2048]{2,1,0:T(8,128)(2,1)} async-done(((bf16[1,128,2048]{2,1,0:T(8,128)(2,1)}), bf16[1,1024,2048]{2,1,0:T(8,128)(2,1)}) %all-gather.6.cloned.1.call-update) | async-done | bytes 4194320 | tf_op jit(solution)/shard_map/all_gather | solution.py:117
  98.6 3.7 %fusion.16 = bf16[1024,128]{1,0:T(8,128)(2,1)S(1)} fusion(bf16[128,2048]{1,0:T(8,128)(2,1)} %all_gather.9, bf16[1,1024,2048]{2,1,0:T(8,128)(2,1)} %all-gather.6.cloned.1.call-done), kind=kOutput, calls=%fused_computation.27 | convolution fusion | flops 537001984 | bytes 4980736 | tf_op jit(solution)/shard_map/dot_general | solution.py:11
  104.0 4.0 %all-to-all-start.6 = ((bf16[8,128,128]{2,1,0:T(8,128)(2,1)}), bf16[8,128,128]{2,1,0:T(8,128)(2,1)}, u32[]{:S(2)}, u32[]{:S(2)}) async-start(bf16[8,128,128]{2,1,0:T(8,128)(2,1)} %bitcast.79), calls=%async_computation.6 | async-start | bytes 524288 | tf_op jit(solution)/shard_map/all_to_all | solution.py:151
  108.1 2.3 %multiply_reduce_fusion.1 = (f32[512]{0:T(512)S(1)}, f32[512]{0:T(512)S(1)}, bf16[512,128]{1,0:T(8,128)(2,1)S(1)}) fusion(bf16[1024,128]{1,0:T(8,128)(2,1)S(1)} %fusion.16, bf16[512,128]{1,0:T(8,128)(2,1)S(1)} %convolution_convert_fusion.1, bf16[1024,128]{1,0:T(8,128)(2,1)S(1)} %bitcast.69, f32[512,1024]{1,0:T(8,128)} %get-tuple-element.13), kind=kOutput, calls=%fused_computation.43 | convolution fusion | flops 135330816 | bytes 2887680 | tf_op jit(solution)/shard_map/dot_general | solution.py:109
  117.6 7.5 %all-to-all-done.6 = bf16[8,128,128]{2,1,0:T(8,128)(2,1)} async-done(((bf16[8,128,128]{2,1,0:T(8,128)(2,1)}), bf16[8,128,128]{2,1,0:T(8,128)(2,1)}, u32[]{:S(2)}, u32[]{:S(2)}) %all-to-all-start.6) | async-done | bytes 262176 | tf_op jit(solution)/shard_map/all_to_all | solution.py:151
  125.1 3.6 %all-to-all-start.5 = ((bf16[8,128,128]{2,1,0:T(8,128)(2,1)}), bf16[8,128,128]{2,1,0:T(8,128)(2,1)S(1)}, u32[]{:S(2)}, u32[]{:S(2)}) async-start(bf16[8,128,128]{2,1,0:T(8,128)(2,1)} %bitcast.25), calls=%async_computation.5 | async-start | bytes 524288 | tf_op jit(solution)/shard_map/all_to_all | solution.py:150
  130.3 8.7 %all-to-all-done.5 = bf16[8,128,128]{2,1,0:T(8,128)(2,1)S(1)} async-done(((bf16[8,128,128]{2,1,0:T(8,128)(2,1)}), bf16[8,128,128]{2,1,0:T(8,128)(2,1)S(1)}, u32[]{:S(2)}, u32[]{:S(2)}) %all-to-all-start.5) | async-done | bytes 262176 | tf_op jit(solution)/shard_map/all_to_all | solution.py:150
  139.0 3.5 %all-to-all-start.4 = ((bf16[8,128,128]{2,1,0:T(8,128)(2,1)}), bf16[8,128,128]{2,1,0:T(8,128)(2,1)S(1)}, u32[]{:S(2)}, u32[]{:S(2)}) async-start(bf16[8,128,128]{2,1,0:T(8,128)(2,1)} %bitcast.23), calls=%async_computation.4 | async-start | bytes 524288 | tf_op jit(solution)/shard_map/all_to_all | solution.py:149
  143.4 15.6 %all-to-all-done.4 = bf16[8,128,128]{2,1,0:T(8,128)(2,1)S(1)} async-done(((bf16[8,128,128]{2,1,0:T(8,128)(2,1)}), bf16[8,128,128]{2,1,0:T(8,128)(2,1)S(1)}, u32[]{:S(2)}, u32[]{:S(2)}) %all-to-all-start.4) | async-done | bytes 262176 | tf_op jit(solution)/shard_map/all_to_all | solution.py:149
  159.0 3.7 %all-to-all-start.3 = ((bf16[8,128,128]{1,2,0:T(8,128)(2,1)}), bf16[8,128,128]{1,2,0:T(8,128)(2,1)S(1)}, u32[]{:S(2)}, u32[]{:S(2)}) async-start(bf16[8,128,128]{1,2,0:T(8,128)(2,1)} %copy.27), calls=%async_computation.3 | async-start | bytes 524288 | tf_op jit(solution)/shard_map/all_to_all | solution.py:112
  168.9 21.6 %all-gather.4.cloned.1.call-done = bf16[1024,2048]{1,0:T(8,128)(2,1)} async-done(((bf16[128,2048]{1,0:T(8,128)(2,1)}), bf16[1024,2048]{1,0:T(8,128)(2,1)}) %all-gather.4.cloned.1.call-update) | async-done | bytes 4194320 | tf_op jit(solution)/shard_map/all_gather | solution.py:114
  190.5 2.9 %fusion.4 = bf16[1,128,2048]{2,1,0:T(8,128)(2,1)S(1)} fusion(bf16[128,1024]{0,1:T(8,128)(2,1)S(1)} %bitcast.78, bf16[1024,2048]{1,0:T(8,128)(2,1)} %all-gather.4.cloned.1.call-done), kind=kOutput, calls=%fused_computation.5 | convolution fusion | flops 537133056 | bytes 4980736 | tf_op jit(solution)/shard_map/dot_general | solution.py:115
  193.6 2.5 %dynamic_update_slice.12 = bf16[1,256,2048]{2,1,0:T(8,128)(2,1)S(1)} dynamic-update-slice(bf16[1,256,2048]{2,1,0:T(8,128)(2,1)S(1)} %broadcast_in_dim.59, bf16[1,128,2048]{2,1,0:T(8,128)(2,1)S(1)} %fusion.4, s32[]{:T(128)} %constant.48.clone.1, s32[]{:T(128)S(6)} %select_n.105, s32[]{:T(128)} %constant.48.clone.1) | dynamic-update-slice | bytes 1048580 | tf_op jit(solution)/shard_map/dynamic_update_slice | solution.py:65
  196.1 21.3 %reduce-scatter.2.cloned.1.call-done = f32[128,512]{1,0:T(8,128)} async-done(((f32[128,2048]{1,0:T(8,128)}), f32[128,512]{1,0:T(8,128)}) %reduce-scatter.2.cloned.1.call-update) | async-done | bytes 262160 | tf_op jit(solution)/shard_map/reduce_scatter | solution.py:122
  (98 shorter events, 25.6 us)
Async XLA Ops:
  7.2 22.0 %copy-start = (bf16[1,256,1024]{2,1,0:T(8,128)(2,1)S(1)}, bf16[1,256,1024]{2,1,0:T(8,128)(2,1)}, u32[]{:S(2)}) copy-start(bf16[1,256,1024]{2,1,0:T(8,128)(2,1)} %param.6) | copy-start | bytes 1572868
  7.2 15.1 %copy-start.17 = (bf16[1,256,1024]{2,1,0:T(8,128)(2,1)S(1)}, bf16[1,256,1024]{2,1,0:T(8,128)(2,1)}, u32[]{:S(2)}) copy-start(bf16[1,256,1024]{2,1,0:T(8,128)(2,1)} %param.7) | copy-start | bytes 1572868
  7.2 15.1 %copy-start.16 = (bf16[1,256,1024]{2,1,0:T(8,128)(2,1)S(1)}, bf16[1,256,1024]{2,1,0:T(8,128)(2,1)}, u32[]{:S(2)}) copy-start(bf16[1,256,1024]{2,1,0:T(8,128)(2,1)} %param.8) | copy-start | bytes 1572868
  7.2 91.4 %all-gather.6.cloned.1.call-start = ((), (), s32[]{:S(2)}) async-start(), calls=%async_computation.10 | async-start | bytes 4718592 | tf_op jit(solution)/shard_map/all_gather | solution.py:117
  12.0 178.6 %all-gather.4.cloned.1.call-start = ((), (), s32[]{:S(2)}) async-start(), calls=%async_computation.8 | async-start | bytes 4718592 | tf_op jit(solution)/shard_map/all_gather | solution.py:114
  22.3 7.4 %copy-start.18 = (s32[1,8]{1,0:T(1,128)S(1)}, s32[1,8]{1,0:T(1,128)}, u32[]{:S(2)}) copy-start(s32[1,8]{1,0:T(1,128)} %param.10) | copy-start | bytes 100
  23.4 22.9 %all-to-all-start.1 = ((bf16[128,8,128]{0,2,1:T(8,128)(2,1)}), bf16[128,8,128]{0,2,1:T(8,128)(2,1)S(1)}, u32[]{:S(2)}, u32[]{:S(2)}) async-start(bf16[128,8,128]{0,2,1:T(8,128)(2,1)} %bitcast.9), calls=%async_computation.1 | async-start | bytes 524288 | tf_op jit(solution)/shard_map/all_to_all | solution.py:75
  46.3 16.6 %all-to-all-start = ((bf16[128,8,128]{0,2,1:T(8,128)(2,1)}), bf16[128,8,128]{0,2,1:T(8,128)(2,1)S(1)}, u32[]{:S(2)}, u32[]{:S(2)}) async-start(bf16[128,8,128]{0,2,1:T(8,128)(2,1)} %bitcast.6), calls=%async_computation | async-start | bytes 524288 | tf_op jit(solution)/shard_map/all_to_all | solution.py:74
  62.8 21.9 %all-to-all-start.2 = ((bf16[128,8,128]{0,2,1:T(8,128)(2,1)}), bf16[128,8,128]{0,2,1:T(8,128)(2,1)S(1)}, u32[]{:S(2)}, u32[]{:S(2)}) async-start(bf16[128,8,128]{0,2,1:T(8,128)(2,1)} %bitcast.12), calls=%async_computation.2 | async-start | bytes 524288 | tf_op jit(solution)/shard_map/all_to_all | solution.py:76
  68.7 18.6 %copy-start.6 = (bf16[4,128,128]{2,1,0:T(8,128)(2,1)}, bf16[4,128,128]{2,1,0:T(8,128)(2,1)S(1)}, u32[]{:S(2)}) copy-start(bf16[4,128,128]{2,1,0:T(8,128)(2,1)S(1)} %copy.26) | copy-start | bytes 393220
  68.9 18.4 %copy-start.14 = (bf16[4,128,128]{2,1,0:T(8,128)(2,1)}, bf16[4,128,128]{2,1,0:T(8,128)(2,1)S(1)}, u32[]{:S(2)}) copy-start(bf16[4,128,128]{2,1,0:T(8,128)(2,1)S(1)} %copy.21) | copy-start | bytes 393220
  98.6 3.7 %copy-start.1 = (f32[512,1024]{1,0:T(8,128)S(1)}, f32[512,1024]{1,0:T(8,128)}, u32[]{:S(2)}) copy-start(f32[512,1024]{1,0:T(8,128)} %get-tuple-element.13) | copy-start | bytes 6291460
  104.0 21.0 %all-to-all-start.6 = ((bf16[8,128,128]{2,1,0:T(8,128)(2,1)}), bf16[8,128,128]{2,1,0:T(8,128)(2,1)}, u32[]{:S(2)}, u32[]{:S(2)}) async-start(bf16[8,128,128]{2,1,0:T(8,128)(2,1)} %bitcast.79), calls=%async_computation.6 | async-start | bytes 524288 | tf_op jit(solution)/shard_map/all_to_all | solution.py:151
  108.1 109.4 %reduce-scatter.2.cloned.1.call-start = ((), (), s32[]{:S(2)}) async-start(), calls=%async_computation.9 | async-start | bytes 1310720 | tf_op jit(solution)/shard_map/reduce_scatter | solution.py:122
  110.4 2.9 %copy-start.8 = (bf16[512,128]{1,0:T(8,128)(2,1)}, bf16[512,128]{1,0:T(8,128)(2,1)S(1)}, u32[]{:S(2)}) copy-start(bf16[512,128]{1,0:T(8,128)(2,1)S(1)} %get-tuple-element.22) | copy-start | bytes 393220
  110.4 2.9 %copy-start.5 = (bf16[1,1024,2048]{2,1,0:T(8,128)(2,1)S(1)}, bf16[1,1024,2048]{2,1,0:T(8,128)(2,1)}, u32[]{:S(2)}) copy-start(bf16[1,1024,2048]{2,1,0:T(8,128)(2,1)} %all-gather.6.cloned.1.call-done) | copy-start | bytes 12582916
  125.1 14.0 %all-to-all-start.5 = ((bf16[8,128,128]{2,1,0:T(8,128)(2,1)}), bf16[8,128,128]{2,1,0:T(8,128)(2,1)S(1)}, u32[]{:S(2)}, u32[]{:S(2)}) async-start(bf16[8,128,128]{2,1,0:T(8,128)(2,1)} %bitcast.25), calls=%async_computation.5 | async-start | bytes 524288 | tf_op jit(solution)/shard_map/all_to_all | solution.py:150
  128.7 13.8 %copy-start.9 = (bf16[512,128]{1,0:T(8,128)(2,1)S(1)}, bf16[512,128]{1,0:T(8,128)(2,1)}, u32[]{:S(2)}) copy-start(bf16[512,128]{1,0:T(8,128)(2,1)} %copy-done.8) | copy-start | bytes 393220
  139.0 20.0 %all-to-all-start.4 = ((bf16[8,128,128]{2,1,0:T(8,128)(2,1)}), bf16[8,128,128]{2,1,0:T(8,128)(2,1)S(1)}, u32[]{:S(2)}, u32[]{:S(2)}) async-start(bf16[8,128,128]{2,1,0:T(8,128)(2,1)} %bitcast.23), calls=%async_computation.4 | async-start | bytes 524288 | tf_op jit(solution)/shard_map/all_to_all | solution.py:149
  159.0 31.6 %all-to-all-start.3 = ((bf16[8,128,128]{1,2,0:T(8,128)(2,1)}), bf16[8,128,128]{1,2,0:T(8,128)(2,1)S(1)}, u32[]{:S(2)}, u32[]{:S(2)}) async-start(bf16[8,128,128]{1,2,0:T(8,128)(2,1)} %copy.27), calls=%async_computation.3 | async-start | bytes 524288 | tf_op jit(solution)/shard_map/all_to_all | solution.py:112
  166.0 27.5 %copy-start.11 = (bf16[1,256,1024]{2,1,0:T(8,128)(2,1)}, bf16[1,256,1024]{2,1,0:T(8,128)(2,1)S(1)}, u32[]{:S(2)}) copy-start(bf16[1,256,1024]{2,1,0:T(8,128)(2,1)S(1)} %dynamic_update_slice.15) | copy-start | bytes 1572868
  167.4 26.0 %copy-start.12 = (bf16[1,256,1024]{2,1,0:T(8,128)(2,1)}, bf16[1,256,1024]{2,1,0:T(8,128)(2,1)S(1)}, u32[]{:S(2)}) copy-start(bf16[1,256,1024]{2,1,0:T(8,128)(2,1)S(1)} %dynamic_update_slice.14) | copy-start | bytes 1572868
  168.9 21.6 %copy-start.13 = (bf16[1,256,1024]{2,1,0:T(8,128)(2,1)}, bf16[1,256,1024]{2,1,0:T(8,128)(2,1)S(1)}, u32[]{:S(2)}) copy-start(bf16[1,256,1024]{2,1,0:T(8,128)(2,1)S(1)} %dynamic_update_slice.13) | copy-start | bytes 1572868
  196.1 21.3 %copy-start.10 = (bf16[1,256,2048]{2,1,0:T(8,128)(2,1)}, bf16[1,256,2048]{2,1,0:T(8,128)(2,1)S(1)}, u32[]{:S(2)}) copy-start(bf16[1,256,2048]{2,1,0:T(8,128)(2,1)S(1)} %dynamic_update_slice.12) | copy-start | bytes 3145732
  (5 other events, 8.4 us)
Sparse Core Ops, SparseCore 0:
  12.1 86.5 all-gather.5
  100.8 89.7 all-gather.3
  193.6 23.7 reduce-scatter.1
where the time goes:
time: 225 us; the launch traced here: 224 us
  waiting for transfers between devices  123 us (55%)
  starting transfers between devices  29.8 us (13%)
  matrix products  20.6 us (9%)
  between operations  15.6 us (7%)
  local copies, waits for them, and re-layouts  13.3 us (6%)
  other arithmetic  11.8 us (5%)
  blocking collectives  10.2 us (5%)
    all_gather x1, waiting for transfers between devices, shards(): full_proj = lax.all_gather(head_rows, 'ctx', axis=0, tiled=True)  21.6 us
    reduce_scatter x1, waiting for transfers between devices, shards(): lax.psum_scatter(weight_term, 'dp', scatter_dimension=1, tiled=True)  21.3 us
    all_to_all x1, waiting for transfers between devices, shards(): lax.all_to_all(v_slot, 'ctx', split_axis=1, concat_axis=0, tiled=True)  15.9 us
    all_to_all x1, waiting for transfers between devices, shards(): lax.all_to_all(k_slot, 'ctx', split_axis=1, concat_axis=0, tiled=True)  15.6 us
    all_to_all x1, waiting for transfers between devices, shards(): lax.all_to_all(q_heads_grad, 'ctx', split_axis=0, concat_axis=1, tiled=True)  15.6 us
    all_to_all x1, waiting for transfers between devices, shards(): lax.all_to_all(q_slot, 'ctx', split_axis=1, concat_axis=0, tiled=True)  12.3 us
    all_gather x1, blocking collectives, shards(): head_rows = lax.all_gather(proj, 'dp', axis=1, tiled=True)  10.2 us
    dot_general x5, matrix products, cross_dot(): lax.dot_general(left_op, right_op, (((1,), (1,)), ((), ())), preferred_el...  8.94 us
  transfers between devices with their start and end apart: 10, of which 9 were waited for; matrix products, arithmetic and copies ran while one was open for 19% of the time, Pallas kernels for 0%

commit v1 on v0

--- a/solution.py
+++ b/solution.py
@@ -146,7 +146,15 @@
     k_heads_grad = (key_grad * score_scale).astype(jnp.bfloat16)
     v_heads_grad = value_grad.astype(jnp.bfloat16)
     q_back, k_back, v_back = (
-        lax.all_to_all(q_heads_grad, "ctx", split_axis=0, concat_axis=1, tiled=True),
+        jnp.concatenate(
+            lax.all_to_all(
+                jnp.stack(jnp.split(q_heads_grad, lax.axis_size("ctx"), axis=0)),
+                axis_name="ctx",
+                split_axis=0,
+                concat_axis=0,
+            ),
+            axis=1,
+        ),
         lax.all_to_all(k_heads_grad, "ctx", split_axis=0, concat_axis=1, tiled=True),
         lax.all_to_all(v_heads_grad, "ctx", split_axis=0, concat_axis=1, tiled=True),
     )

time: 225 us -> 227 us (level)
  local copies, waits for them, and re-layouts: 13.3 us -> 21.2 us
  matrix products: 20.6 us -> 16.8 us
  blocking collectives: 10.2 us -> 7.62 us
    all_gather x1, waiting for transfers between devices: 4.03 us -> 16.9 us  [shards(): part_rows = lax.all_gather(g_slot, 'ctx', axis=0, tiled=True)]
    all_to_all x1, waiting for transfers between devices: 15.6 us -> 5.75 us  [shards(): lax.all_to_all(k_slot, 'ctx', split_axis=1, concat_axis=0, tiled=True)]
    unnamed x41 -> x48, local copies, waits for them, and re-layouts: 1.31 us -> 7.58 us
    all_gather x1, blocking collectives: 10.2 us -> 7.62 us  [shards(): head_rows = lax.all_gather(proj, 'dp', axis=1, tiled=True)]
where the time goes in v1:
time: 227 us; the launch traced here: 226 us
  waiting for transfers between devices  123 us (54%)
  starting transfers between devices  30.8 us (14%)
  local copies, waits for them, and re-layouts  21.2 us (9%)
  matrix products  16.8 us (7%)
  between operations  15.6 us (7%)
  other arithmetic  10.1 us (4%)
  blocking collectives  7.62 us (3%)
    all_gather x1, waiting for transfers between devices, shards(): full_proj = lax.all_gather(head_rows, 'ctx', axis=0, tiled=True)  22.1 us
    reduce_scatter x1, waiting for transfers between devices, shards(): lax.psum_scatter(weight_term, 'dp', scatter_dimension=1, tiled=True)  21.3 us
    all_gather x1, waiting for transfers between devices, shards(): part_rows = lax.all_gather(g_slot, 'ctx', axis=0, tiled=True)  16.9 us
    all_to_all x1, waiting for transfers between devices, shards(): lax.all_to_all(jnp.stack(jnp.split(q_heads_grad, lax.axis_size('ctx'), ax...  15.8 us
    all_to_all x1, waiting for transfers between devices, shards(): lax.all_to_all(v_slot, 'ctx', split_axis=1, concat_axis=0, tiled=True)  15.2 us
    all_to_all x1, waiting for transfers between devices, shards(): lax.all_to_all(q_slot, 'ctx', split_axis=1, concat_axis=0, tiled=True)  11.3 us
    all_to_all x1, waiting for transfers between devices, shards(): lax.all_to_all(k_heads_grad, 'ctx', split_axis=0, concat_axis=1, tiled=True)  9.75 us
    all_gather x1, blocking collectives, shards(): head_rows = lax.all_gather(proj, 'dp', axis=1, tiled=True)  7.62 us
  transfers between devices with their start and end apart: 10, of which 9 were waited for; matrix products, arithmetic and copies ran while one was open for 19% of the time, Pallas kernels for 0%

profile of v1, /device:TPU:0, one launch (start us, length us, event | category | flops | bytes accessed | tf_op | source)
XLA Modules:
  0.0 225.6 jit_solution(16885216155797415011)
XLA Ops:
  9.9 2.0 dynamic-slice_select_fusion
  14.0 7.3 %all-to-all-start.1 = ((bf16[128,8,128]{0,2,1:T(8,128)(2,1)}), bf16[128,8,128]{0,2,1:T(8,128)(2,1)S(1)}, u32[]{:S(2)}, u32[]{:S(2)}) async-start(bf16[128,8,128]{0,2,1:T(8,128)(2,1)} %bitcast.9), calls=%async_computation.1 | async-start | bytes 524288 | tf_op jit(solution)/shard_map/all_to_all | solution.py:75
  21.4 7.6 %all_gather.9 = bf16[128,2048]{1,0:T(8,128)(2,1)} all-gather(bf16[128,512]{1,0:T(8,128)(2,1)S(1)} %copy-done.17), channel_id=1, replica_groups=mesh['dp'=4,'ctx'=8] {'dp'}, dimensions={1}, use_global_device_ids=true | all-gather | bytes 655360 | tf_op jit(solution)/shard_map/all_gather | solution.py:113
  30.5 5.7 %all-to-all-done.1 = bf16[128,8,128]{0,2,1:T(8,128)(2,1)S(1)} async-done(((bf16[128,8,128]{0,2,1:T(8,128)(2,1)}), bf16[128,8,128]{0,2,1:T(8,128)(2,1)S(1)}, u32[]{:S(2)}, u32[]{:S(2)}) %all-to-all-start.1) | async-done | bytes 262176 | tf_op jit(solution)/shard_map/all_to_all | solution.py:75
  36.2 4.4 %all-to-all-start = ((bf16[128,8,128]{0,2,1:T(8,128)(2,1)}), bf16[128,8,128]{0,2,1:T(8,128)(2,1)S(1)}, u32[]{:S(2)}, u32[]{:S(2)}) async-start(bf16[128,8,128]{0,2,1:T(8,128)(2,1)} %bitcast.6), calls=%async_computation | async-start | bytes 524288 | tf_op jit(solution)/shard_map/all_to_all | solution.py:74
  41.5 11.3 %all-to-all-done = bf16[128,8,128]{0,2,1:T(8,128)(2,1)S(1)} async-done(((bf16[128,8,128]{0,2,1:T(8,128)(2,1)}), bf16[128,8,128]{0,2,1:T(8,128)(2,1)S(1)}, u32[]{:S(2)}, u32[]{:S(2)}) %all-to-all-start) | async-done | bytes 262176 | tf_op jit(solution)/shard_map/all_to_all | solution.py:74
  52.7 3.6 %all-to-all-start.2 = ((bf16[128,8,128]{0,2,1:T(8,128)(2,1)}), bf16[128,8,128]{0,2,1:T(8,128)(2,1)S(1)}, u32[]{:S(2)}, u32[]{:S(2)}) async-start(bf16[128,8,128]{0,2,1:T(8,128)(2,1)} %bitcast.12), calls=%async_computation.2 | async-start | bytes 524288 | tf_op jit(solution)/shard_map/all_to_all | solution.py:76
  56.9 15.2 %all-to-all-done.2 = bf16[128,8,128]{0,2,1:T(8,128)(2,1)S(1)} async-done(((bf16[128,8,128]{0,2,1:T(8,128)(2,1)}), bf16[128,8,128]{0,2,1:T(8,128)(2,1)S(1)}, u32[]{:S(2)}, u32[]{:S(2)}) %all-to-all-start.2) | async-done | bytes 262176 | tf_op jit(solution)/shard_map/all_to_all | solution.py:76
  72.7 1.9 fusion.7
  74.6 3.0 %fusion.11 = (f32[512]{0:T(512)S(1)}, f32[512]{0:T(512)S(1)}) fusion(f32[512,1024]{1,0:T(8,128)S(1)} %get-tuple-element.21, f32[512]{0:T(512)S(1)} %get-tuple-element.9, s32[512]{0:T(512)S(1)} %slice.46, s32[512]{0:T(512)S(1)} %get-tuple-element.16, s32[1024]{0:T(1024)S(1)} %get-tuple-element.19, pred[1024]{0:T(1024)(128)(4,1)S(1)} %broadcast_bitcast_fusion, ...), kind=kLoop, calls=%fused_computation.22 | loop fusion | flops 10484736 | bytes 4216832 | tf_op jit(solution)/shard_map/reduce_sum | solution.py:40
  77.6 2.8 %fusion.10 = (f32[512,1024]{1,0:T(8,128)S(1)}, f32[512,1024]{1,0:T(8,128)S(1)}) fusion(f32[512,1024]{1,0:T(8,128)S(1)} %get-tuple-element.21, f32[512]{0:T(512)S(1)} %get-tuple-element.7, f32[512]{0:T(512)S(1)} %get-tuple-element.9, s32[512]{0:T(512)S(1)} %slice.46, s32[512]{0:T(512)S(1)} %get-tuple-element.16, s32[1024]{0:T(1024)S(1)} %get-tuple-element.19, ...), kind=kLoop, calls=%fused_computation.21 | loop fusion | flops 10485760 | bytes 8411136 | tf_op jit(solution)/shard_map/div | solution.py:40
  82.2 16.9 %all-gather.6.cloned.1.call-done = bf16[1,1024,2048]{2,1,0:T(8,128)(2,1)} async-done(((bf16[1,128,2048]{2,1,0:T(8,128)(2,1)}), bf16[1,1024,2048]{2,1,0:T(8,128)(2,1)}) %all-gather.6.cloned.1.call-update) | async-done | bytes 4194320 | tf_op jit(solution)/shard_map/all_gather | solution.py:117
  99.2 3.7 %fusion.16 = bf16[1024,128]{1,0:T(8,128)(2,1)S(1)} fusion(bf16[128,2048]{1,0:T(8,128)(2,1)} %all_gather.9, bf16[1,1024,2048]{2,1,0:T(8,128)(2,1)} %all-gather.6.cloned.1.call-done), kind=kOutput, calls=%fused_computation.27 | convolution fusion | flops 537001984 | bytes 4980736 | tf_op jit(solution)/shard_map/dot_general | solution.py:11
  104.6 4.0 %all-to-all-start.6 = ((bf16[8,128,128]{2,1,0:T(8,128)(2,1)}), bf16[8,128,128]{2,1,0:T(8,128)(2,1)}, u32[]{:S(2)}, u32[]{:S(2)}) async-start(bf16[8,128,128]{2,1,0:T(8,128)(2,1)} %bitcast.110), calls=%async_computation.6 | async-start | bytes 524288 | tf_op jit(solution)/shard_map/all_to_all | solution.py:159
  119.1 5.4 %all-to-all-done.6 = bf16[8,128,128]{2,1,0:T(8,128)(2,1)} async-done(((bf16[8,128,128]{2,1,0:T(8,128)(2,1)}), bf16[8,128,128]{2,1,0:T(8,128)(2,1)}, u32[]{:S(2)}, u32[]{:S(2)}) %all-to-all-start.6) | async-done | bytes 262176 | tf_op jit(solution)/shard_map/all_to_all | solution.py:159
  124.5 4.1 %all-to-all-start.5 = ((bf16[8,128,128]{2,1,0:T(8,128)(2,1)}), bf16[8,128,128]{2,1,0:T(8,128)(2,1)S(1)}, u32[]{:S(2)}, u32[]{:S(2)}) async-start(bf16[8,128,128]{2,1,0:T(8,128)(2,1)} %bitcast.33), calls=%async_computation.5 | async-start | bytes 524288 | tf_op jit(solution)/shard_map/all_to_all | solution.py:158
  130.4 9.8 %all-to-all-done.5 = bf16[8,128,128]{2,1,0:T(8,128)(2,1)S(1)} async-done(((bf16[8,128,128]{2,1,0:T(8,128)(2,1)}), bf16[8,128,128]{2,1,0:T(8,128)(2,1)S(1)}, u32[]{:S(2)}, u32[]{:S(2)}) %all-to-all-start.5) | async-done | bytes 262176 | tf_op jit(solution)/shard_map/all_to_all | solution.py:158
  140.2 3.6 %all-to-all-start.4 = ((bf16[8,128,128]{2,1,0:T(8,128)(2,1)}), bf16[8,128,128]{2,1,0:T(8,128)(2,1)S(1)}, u32[]{:S(2)}, u32[]{:S(2)}) async-start(bf16[8,128,128]{2,1,0:T(8,128)(2,1)} %fusion.30), calls=%async_computation.4 | async-start | bytes 524288 | tf_op jit(solution)/shard_map/all_to_all | solution.py:150
  144.7 15.8 %all-to-all-done.4 = bf16[8,128,128]{2,1,0:T(8,128)(2,1)S(1)} async-done(((bf16[8,128,128]{2,1,0:T(8,128)(2,1)}), bf16[8,128,128]{2,1,0:T(8,128)(2,1)S(1)}, u32[]{:S(2)}, u32[]{:S(2)}) %all-to-all-start.4) | async-done | bytes 262176 | tf_op jit(solution)/shard_map/all_to_all | solution.py:150
  160.5 3.4 %all-to-all-start.3 = ((bf16[8,128,128]{1,2,0:T(8,128)(2,1)}), bf16[8,128,128]{1,2,0:T(8,128)(2,1)S(1)}, u32[]{:S(2)}, u32[]{:S(2)}) async-start(bf16[8,128,128]{1,2,0:T(8,128)(2,1)} %copy.27), calls=%async_computation.3 | async-start | bytes 524288 | tf_op jit(solution)/shard_map/all_to_all | solution.py:112
  170.1 22.1 %all-gather.4.cloned.1.call-done = bf16[1024,2048]{1,0:T(8,128)(2,1)} async-done(((bf16[128,2048]{1,0:T(8,128)(2,1)}), bf16[1024,2048]{1,0:T(8,128)(2,1)}) %all-gather.4.cloned.1.call-update) | async-done | bytes 4194320 | tf_op jit(solution)/shard_map/all_gather | solution.py:114
  192.2 2.9 %fusion.4 = bf16[1,128,2048]{2,1,0:T(8,128)(2,1)S(1)} fusion(bf16[128,1024]{0,1:T(8,128)(2,1)S(1)} %bitcast.111, bf16[1024,2048]{1,0:T(8,128)(2,1)} %all-gather.4.cloned.1.call-done), kind=kOutput, calls=%fused_computation.5 | convolution fusion | flops 537133056 | bytes 4980736 | tf_op jit(solution)/shard_map/dot_general | solution.py:115
  195.3 2.5 %dynamic_update_slice.12 = bf16[1,256,2048]{2,1,0:T(8,128)(2,1)S(1)} dynamic-update-slice(bf16[1,256,2048]{2,1,0:T(8,128)(2,1)S(1)} %broadcast_in_dim.56, bf16[1,128,2048]{2,1,0:T(8,128)(2,1)S(1)} %fusion.4, s32[]{:T(128)} %constant.48.clone.1, s32[]{:T(128)S(6)} %select_n.105, s32[]{:T(128)} %constant.48.clone.1) | dynamic-update-slice | bytes 1048580 | tf_op jit(solution)/shard_map/dynamic_update_slice | solution.py:65
  197.8 21.3 %reduce-scatter.2.cloned.1.call-done = f32[128,512]{1,0:T(8,128)} async-done(((f32[128,2048]{1,0:T(8,128)}), f32[128,512]{1,0:T(8,128)}) %reduce-scatter.2.cloned.1.call-update) | async-done | bytes 262160 | tf_op jit(solution)/shard_map/reduce_scatter | solution.py:122
  (105 shorter events, 29.6 us)
Async XLA Ops:
  7.2 21.9 %copy-start = (bf16[1,256,1024]{2,1,0:T(8,128)(2,1)S(1)}, bf16[1,256,1024]{2,1,0:T(8,128)(2,1)}, u32[]{:S(2)}) copy-start(bf16[1,256,1024]{2,1,0:T(8,128)(2,1)} %param.6) | copy-start | bytes 1572868
  7.2 92.0 %all-gather.6.cloned.1.call-start = ((), (), s32[]{:S(2)}) async-start(), calls=%async_computation.10 | async-start | bytes 4718592 | tf_op jit(solution)/shard_map/all_gather | solution.py:117
  9.9 11.5 %copy-start.17 = (bf16[128,512]{1,0:T(8,128)(2,1)S(1)}, bf16[128,512]{1,0:T(8,128)(2,1)}, u32[]{:S(2)}) copy-start(bf16[128,512]{1,0:T(8,128)(2,1)} %param.11) | copy-start | bytes 393220
  11.9 17.1 %copy-start.18 = (s32[1,8]{1,0:T(1,128)S(1)}, s32[1,8]{1,0:T(1,128)}, u32[]{:S(2)}) copy-start(s32[1,8]{1,0:T(1,128)} %param.10) | copy-start | bytes 100
  14.0 22.2 %all-to-all-start.1 = ((bf16[128,8,128]{0,2,1:T(8,128)(2,1)}), bf16[128,8,128]{0,2,1:T(8,128)(2,1)S(1)}, u32[]{:S(2)}, u32[]{:S(2)}) async-start(bf16[128,8,128]{0,2,1:T(8,128)(2,1)} %bitcast.9), calls=%async_computation.1 | async-start | bytes 524288 | tf_op jit(solution)/shard_map/all_to_all | solution.py:75
  21.4 170.8 %all-gather.4.cloned.1.call-start = ((), (), s32[]{:S(2)}) async-start(), calls=%async_computation.8 | async-start | bytes 4718592 | tf_op jit(solution)/shard_map/all_gather | solution.py:114
  36.2 16.5 %all-to-all-start = ((bf16[128,8,128]{0,2,1:T(8,128)(2,1)}), bf16[128,8,128]{0,2,1:T(8,128)(2,1)S(1)}, u32[]{:S(2)}, u32[]{:S(2)}) async-start(bf16[128,8,128]{0,2,1:T(8,128)(2,1)} %bitcast.6), calls=%async_computation | async-start | bytes 524288 | tf_op jit(solution)/shard_map/all_to_all | solution.py:74
  52.7 19.3 %all-to-all-start.2 = ((bf16[128,8,128]{0,2,1:T(8,128)(2,1)}), bf16[128,8,128]{0,2,1:T(8,128)(2,1)S(1)}, u32[]{:S(2)}, u32[]{:S(2)}) async-start(bf16[128,8,128]{0,2,1:T(8,128)(2,1)} %bitcast.12), calls=%async_computation.2 | async-start | bytes 524288 | tf_op jit(solution)/shard_map/all_to_all | solution.py:76
  56.7 17.9 %copy-start.5 = (bf16[4,128,128]{2,1,0:T(8,128)(2,1)}, bf16[4,128,128]{2,1,0:T(8,128)(2,1)S(1)}, u32[]{:S(2)}) copy-start(bf16[4,128,128]{2,1,0:T(8,128)(2,1)S(1)} %copy.26) | copy-start | bytes 393220
  56.9 17.7 %copy-start.15 = (bf16[4,128,128]{2,1,0:T(8,128)(2,1)}, bf16[4,128,128]{2,1,0:T(8,128)(2,1)S(1)}, u32[]{:S(2)}) copy-start(bf16[4,128,128]{2,1,0:T(8,128)(2,1)S(1)} %copy.21) | copy-start | bytes 393220
  99.2 3.7 %copy-start.2 = (f32[512,1024]{1,0:T(8,128)S(1)}, f32[512,1024]{1,0:T(8,128)}, u32[]{:S(2)}) copy-start(f32[512,1024]{1,0:T(8,128)} %copy-done.1) | copy-start | bytes 6291460
  104.6 20.0 %all-to-all-start.6 = ((bf16[8,128,128]{2,1,0:T(8,128)(2,1)}), bf16[8,128,128]{2,1,0:T(8,128)(2,1)}, u32[]{:S(2)}, u32[]{:S(2)}) async-start(bf16[8,128,128]{2,1,0:T(8,128)(2,1)} %bitcast.110), calls=%async_computation.6 | async-start | bytes 524288 | tf_op jit(solution)/shard_map/all_to_all | solution.py:159
  108.6 110.5 %reduce-scatter.2.cloned.1.call-start = ((), (), s32[]{:S(2)}) async-start(), calls=%async_computation.9 | async-start | bytes 1310720 | tf_op jit(solution)/shard_map/reduce_scatter | solution.py:122
  109.4 6.0 %copy-start.7 = (bf16[512,128]{1,0:T(8,128)(2,1)}, bf16[512,128]{1,0:T(8,128)(2,1)S(1)}, u32[]{:S(2)}) copy-start(bf16[512,128]{1,0:T(8,128)(2,1)S(1)} %get-tuple-element.22) | copy-start | bytes 393220
  113.2 2.2 copy-start.4
  115.4 1.8 copy-start.14
  117.2 26.6 %copy-start.8 = (bf16[512,128]{1,0:T(8,128)(2,1)S(1)}, bf16[512,128]{1,0:T(8,128)(2,1)}, u32[]{:S(2)}) copy-start(bf16[512,128]{1,0:T(8,128)(2,1)} %copy-done.7) | copy-start | bytes 393220
  124.5 15.7 %all-to-all-start.5 = ((bf16[8,128,128]{2,1,0:T(8,128)(2,1)}), bf16[8,128,128]{2,1,0:T(8,128)(2,1)S(1)}, u32[]{:S(2)}, u32[]{:S(2)}) async-start(bf16[8,128,128]{2,1,0:T(8,128)(2,1)} %bitcast.33), calls=%async_computation.5 | async-start | bytes 524288 | tf_op jit(solution)/shard_map/all_to_all | solution.py:158
  140.2 20.3 %all-to-all-start.4 = ((bf16[8,128,128]{2,1,0:T(8,128)(2,1)}), bf16[8,128,128]{2,1,0:T(8,128)(2,1)S(1)}, u32[]{:S(2)}, u32[]{:S(2)}) async-start(bf16[8,128,128]{2,1,0:T(8,128)(2,1)} %fusion.30), calls=%async_computation.4 | async-start | bytes 524288 | tf_op jit(solution)/shard_map/all_to_all | solution.py:150
  160.5 31.7 %all-to-all-start.3 = ((bf16[8,128,128]{1,2,0:T(8,128)(2,1)}), bf16[8,128,128]{1,2,0:T(8,128)(2,1)S(1)}, u32[]{:S(2)}, u32[]{:S(2)}) async-start(bf16[8,128,128]{1,2,0:T(8,128)(2,1)} %copy.27), calls=%async_computation.3 | async-start | bytes 524288 | tf_op jit(solution)/shard_map/all_to_all | solution.py:112
  167.2 27.9 %copy-start.10 = (bf16[1,256,1024]{2,1,0:T(8,128)(2,1)}, bf16[1,256,1024]{2,1,0:T(8,128)(2,1)S(1)}, u32[]{:S(2)}) copy-start(bf16[1,256,1024]{2,1,0:T(8,128)(2,1)S(1)} %dynamic_update_slice.15) | copy-start | bytes 1572868
  168.7 26.5 %copy-start.11 = (bf16[1,256,1024]{2,1,0:T(8,128)(2,1)}, bf16[1,256,1024]{2,1,0:T(8,128)(2,1)S(1)}, u32[]{:S(2)}) copy-start(bf16[1,256,1024]{2,1,0:T(8,128)(2,1)S(1)} %dynamic_update_slice.14) | copy-start | bytes 1572868
  170.1 22.1 %copy-start.12 = (bf16[1,256,1024]{2,1,0:T(8,128)(2,1)}, bf16[1,256,1024]{2,1,0:T(8,128)(2,1)S(1)}, u32[]{:S(2)}) copy-start(bf16[1,256,1024]{2,1,0:T(8,128)(2,1)S(1)} %dynamic_update_slice.13) | copy-start | bytes 1572868
  197.8 21.3 %copy-start.9 = (bf16[1,256,2048]{2,1,0:T(8,128)(2,1)}, bf16[1,256,2048]{2,1,0:T(8,128)(2,1)S(1)}, u32[]{:S(2)}) copy-start(bf16[1,256,2048]{2,1,0:T(8,128)(2,1)S(1)} %dynamic_update_slice.12) | copy-start | bytes 3145732
  (5 other events, 6.7 us)
Sparse Core Ops, SparseCore 0:
  12.1 87.0 all-gather.5
  101.3 90.8 all-gather.3
  195.3 23.7 reduce-scatter.1
